TPU v7x, 32 devices: a whole 2x2x4 slice. The times are simulated.
32 devices in a mesh: shard: 4 (over z), tensor: 4 (over x, core), section: 2 (over y).
Axes of the slice: x: 2, y: 2, z: 4, core: 2. Of those that a mesh axis runs over, the one named last changes fastest.
Arguments:
- hidden_acts: bfloat16 [2, 10240, 4096], P('section', 'shard', 'tensor'), may hold values from -8 to 8
- out_grads: bfloat16 [2, 10240, 1024], P('section', 'shard'), may hold values from -8 to 8
- errors: float32 [2, 4, 1024, 4096], P('section', 'shard', None, 'tensor'), may hold values from -3 to 3
- factors: float32 [2, 32, 4096], P('section', None, 'tensor'), may hold values from -6 to 6
- whiten: float32 [2, 2, 32, 32], P('section'), may hold values from -1.5 to 3
- momentum: float32 [2, 1024, 4096], P('section', 'shard', 'tensor'), may hold values from -3 to 3
- master: float32 [2, 1024, 4096], P('section', 'shard', 'tensor'), may hold values from -3 to 3
- table: bfloat16 [32768, 1024], P(('shard', 'section'), 'tensor'), may hold values from -5 to 5
- touched_ids: int32 [1024], P(('shard', 'section')), may hold values from 0 to 32767, as said below
- touched_grads: bfloat16 [1024, 1024], P(('shard', 'section'), 'tensor'), may hold values from -5 to 5
Outputs:
- new_errors: float32 [2, 4, 1024, 4096], P('section', 'shard', None, 'tensor')
- new_factors: float32 [2, 32, 4096], P('section', None, 'tensor')
- new_momentum: float32 [2, 1024, 4096], P('section', 'shard', 'tensor')
- new_master: float32 [2, 1024, 4096], P('section', 'shard', 'tensor')
- new_weights: bfloat16 [2, 1024, 4096], P('section', None, 'tensor')
- new_table: bfloat16 [32768, 1024], P(('shard', 'section'), 'tensor')
Inputs may be any that keep to these rules, and one draw needn't show every extreme that they name: `touched_ids`: the 128 ids of one device of shard and section name at most 32 rows in each block of 4096 vocabulary rows; in every draw one block receives exactly 32 rows from every device.
All inputs are finite; a program needn't handle non-finite values.
Results may differ from a plain program's by a relative error of at most 0.0036.
Values may be sent and summed in bfloat16 or wider, within the bound.
A program may use at most 128 MiB of HBM per device.

v0:
```python
import jax
import jax.numpy as jnp
from jax import lax
from jax.sharding import PartitionSpec as P

D = 1024
FF = 4096
ROUNDS = 2
epsilon = 1e-06
momentum_decay = 0.9
learn_rate = 0.1
embed_rate = 0.25
clip_level = 0.03
highest = lax.Precision.HIGHEST


def on_device(
    hidden_acts,
    out_grads,
    errors,
    factors,
    whiten,
    momentum,
    master,
    table,
    touched_ids,
    touched_grads,
):
    shards = lax.axis_size("shard")
    grad_block = lax.dot_general(
        out_grads[0], hidden_acts[0], (((0,), (0,)), ((), ())), preferred_element_type=jnp.float32
    )
    rounded = lax.optimization_barrier(grad_block.astype(jnp.bfloat16))
    corrected = rounded.astype(jnp.float32) + errors[0, 0]
    right_part = factors[0]
    rank_count = right_part.shape[0]
    left_unit = None
    for power_round in range(ROUNDS):
        left_part = lax.dot_general(
            right_part,
            corrected,
            (((1,), (1,)), ((), ())),
            precision=highest,
            preferred_element_type=jnp.float32,
        )
        left_sum = lax.psum(left_part, ("shard", "tensor"))
        whitened = jnp.dot(whiten[0, power_round].T, left_sum, precision=highest)
        scaling = lax.rsqrt(jnp.sum(whitened * whitened) / rank_count + epsilon)
        left_unit = whitened * scaling
        right_local = jnp.dot(left_unit, corrected, precision=highest)
        right_part = lax.psum(right_local, "shard") / shards
    gram_left = jnp.dot(left_unit, left_unit.T, precision=highest)
    gram_right = jnp.dot(right_part, right_part.T, precision=highest)
    total_squares = lax.psum(jnp.sum(gram_left * gram_right), ("tensor", "section"))
    approx = lax.dot_general(
        left_unit,
        right_part,
        (((0,), (0,)), ((), ())),
        precision=highest,
        preferred_element_type=jnp.float32,
    )
    new_errors = (corrected - approx)[None, None]
    entries = lax.axis_size("section") * D * FF
    spread = jnp.sqrt(total_squares / entries + epsilon)
    clip_factor = jnp.minimum(1.0, clip_level / spread)
    rows_own = momentum.shape[1]
    row_start = lax.axis_index("shard") * rows_own
    approx_rows = lax.dynamic_slice_in_dim(approx, row_start, rows_own, 0)
    new_momentum = momentum_decay * momentum + clip_factor * approx_rows[None]
    new_master = master - learn_rate * new_momentum
    new_weights = lax.all_gather(new_master.astype(jnp.bfloat16), "shard", axis=1, tiled=True)
    new_factors = right_part[None]
    vocab_rows = table.shape[0]
    table_width = table.shape[1]
    first_row = lax.axis_index(("shard", "section")) * vocab_rows
    recv_rows, recv_ids = (
        lax.all_gather(touched_grads, ("shard", "section"), axis=0, tiled=True),
        lax.all_gather(touched_ids, ("shard", "section"), axis=0, tiled=True),
    )
    local_index = recv_ids - first_row
    inside = (local_index >= 0) & (local_index < vocab_rows)
    target = jnp.where(inside, local_index, vocab_rows)
    table_grad = (
        jnp.zeros((vocab_rows, table_width), jnp.float32)
        .at[target]
        .add(recv_rows.astype(jnp.float32), mode="drop")
    )
    new_table = (table.astype(jnp.float32) - embed_rate * table_grad).astype(jnp.bfloat16)
    return (new_errors, new_factors, new_momentum, new_master, new_weights, new_table)


def solution(mesh):
    in_specs = (
        P("section", "shard", "tensor"),
        P("section", "shard", None),
        P("section", "shard", None, "tensor"),
        P("section", None, "tensor"),
        P("section", None, None, None),
        P("section", "shard", "tensor"),
        P("section", "shard", "tensor"),
        P(("shard", "section"), "tensor"),
        P(("shard", "section")),
        P(("shard", "section"), "tensor"),
    )
    out_specs = (
        P("section", "shard", None, "tensor"),
        P("section", None, "tensor"),
        P("section", "shard", "tensor"),
        P("section", "shard", "tensor"),
        P("section", None, "tensor"),
        P(("shard", "section"), "tensor"),
    )
    return jax.shard_map(
        on_device, mesh=mesh, in_specs=in_specs, out_specs=out_specs, check_vma=False
    )
```

profile of v0, /device:TPU:0, one launch (start us, length us, event | category | flops | bytes accessed | tf_op | source)
XLA Modules:
  0.0 398.0 jit_solution(17824651592674097183)
XLA Ops:
  7.2 0.0 copy-start
  7.2 0.0 all-reduce.5.cloned.1.call-start
  7.2 0.0 copy-start.1
  7.2 9.3 %fusion.5 = bf16[1024,1024]{1,0:T(8,128)(2,1)S(1)} fusion(bf16[1,2560,1024]{2,1,0:T(8,128)(2,1)} %param.10, bf16[1,2560,1024]{2,1,0:T(8,128)(2,1)} %param.11), kind=kOutput, calls=%fused_computation.9 | convolution fusion | flops 5369757696 | bytes 12582912 | tf_op jit(solution)/shard_map/dot_general | solution.py:30
  16.5 0.0 copy-done
  16.5 0.0 copy-done.1
  16.5 0.0 copy-start.9
  16.6 4.7 %convolution_bitcast_fusion = f32[32,1024]{1,0:T(8,128)} fusion(f32[1,32,1024]{2,1,0:T(8,128)S(1)} %copy-done, f32[1,1,1024,1024]{3,2,1,0:T(8,128)S(1)} %copy-done.1, bf16[1024,1024]{1,0:T(8,128)(2,1)S(1)} %fusion.5), kind=kOutput, calls=%fused_computation.10 | convolution fusion | flops 404750336 | bytes 6553600 | tf_op jit(solution)/shard_map/dot_general | solution.py:39
  21.2 0.0 all-reduce.5.cloned.1.call-update
  21.3 0.0 all-reduce.7.cloned.1.call-start
  21.3 89.8 %all-reduce.5.cloned.1.call-done = f32[32,1024]{1,0:T(8,128)} async-done(((f32[32,1024]{1,0:T(8,128)}), f32[32,1024]{1,0:T(8,128)}) %all-reduce.5.cloned.1.call-update) | async-done | bytes 131088 | tf_op jit(solution)/shard_map/psum | solution.py:46
  111.1 0.0 copy-done.9
  111.1 1.8 multiply_reduce_fusion.1
  113.7 5.6 %fusion.15 = f32[32,1024]{1,0:T(8,128)} fusion(f32[1024,32]{0,1:T(8,128)S(1)} %get-tuple-element.10, f32[]{:T(128)S(6)} %rsqrt.7, f32[1,1,1024,1024]{3,2,1,0:T(8,128)} %param.12, bf16[1024,1024]{1,0:T(8,128)(2,1)S(1)} %fusion.5), kind=kOutput, calls=%fused_computation.20 | convolution fusion | flops 404783104 | bytes 6553604 | tf_op jit(solution)/shard_map/dot_general | solution.py:50
  119.2 0.0 all-reduce.7.cloned.1.call-update
  119.2 0.0 all-reduce.9.cloned.1.call-start
  119.3 36.2 %all-reduce.7.cloned.1.call-done = f32[32,1024]{1,0:T(8,128)} async-done(((f32[32,1024]{1,0:T(8,128)}), f32[32,1024]{1,0:T(8,128)}) %all-reduce.7.cloned.1.call-update) | async-done | bytes 131088 | tf_op jit(solution)/shard_map/psum | solution.py:51
  155.5 6.8 %fusion.13 = f32[32,1024]{1,0:T(8,128)} fusion(f32[32,1024]{1,0:T(8,128)} %all-reduce.7.cloned.1.call-done, f32[1,1,1024,1024]{3,2,1,0:T(8,128)} %param.12, bf16[1024,1024]{1,0:T(8,128)(2,1)S(1)} %fusion.5), kind=kOutput, calls=%fused_computation.18 | convolution fusion | flops 404783104 | bytes 6553600 | tf_op jit(solution)/shard_map/dot_general | solution.py:39
  162.2 0.0 all-reduce.9.cloned.1.call-update
  162.3 0.2 all-reduce.11.cloned.1.call-start
  162.5 86.6 %all-reduce.9.cloned.1.call-done = f32[32,1024]{1,0:T(8,128)} async-done(((f32[32,1024]{1,0:T(8,128)}), f32[32,1024]{1,0:T(8,128)}) %all-reduce.9.cloned.1.call-update) | async-done | bytes 131088 | tf_op jit(solution)/shard_map/psum | solution.py:46
  249.1 1.8 multiply_reduce_fusion
  251.6 0.0 copy-start.6
  251.6 5.6 %fusion.23 = f32[32,1024]{1,0:T(8,128)} fusion(f32[1024,32]{0,1:T(8,128)S(1)} %get-tuple-element.12, f32[]{:T(128)S(6)} %rsqrt.8, f32[1,1,1024,1024]{3,2,1,0:T(8,128)} %param.12, bf16[1024,1024]{1,0:T(8,128)(2,1)S(1)} %fusion.5), kind=kOutput, calls=%fused_computation.30 | convolution fusion | flops 404783104 | bytes 6553604 | tf_op jit(solution)/shard_map/dot_general | solution.py:50
  257.2 0.0 all-reduce.11.cloned.1.call-update
  257.3 0.0 all-gather.3.cloned.1.call-start
  257.3 0.2 fusion.20
  257.6 36.0 %all-reduce.11.cloned.1.call-done = f32[32,1024]{1,0:T(8,128)} async-done(((f32[32,1024]{1,0:T(8,128)}), f32[32,1024]{1,0:T(8,128)}) %all-reduce.11.cloned.1.call-update) | async-done | bytes 131088 | tf_op jit(solution)/shard_map/psum | solution.py:51
  293.6 1.8 fusion.11
  295.4 14.0 %psum.39 = f32[]{:T(128)} all-reduce(f32[]{:T(128)} %fusion.11), channel_id=1, replica_groups=mesh['shard'=4,'tensor'=4,'section'=2] {'tensor','section'}, use_global_device_ids=true, to_apply=%region_7.0 | all-reduce | flops 1 | bytes 8 | tf_op jit(solution)/shard_map/psum | solution.py:54
  310.1 0.0 copy-start.7
  310.1 4.5 %fusion.18 = f32[1024,1024]{1,0:T(8,128)S(1)} fusion(f32[32,1024]{1,0:T(8,128)} %all-reduce.11.cloned.1.call-done, f32[1024,32]{0,1:T(8,128)S(1)} %get-tuple-element.12, f32[]{:T(128)S(6)} %rsqrt.8), kind=kOutput, calls=%fused_computation.25 | convolution fusion | flops 402718720 | bytes 4456452 | tf_op jit(solution)/shard_map/dot_general | solution.py:55
  314.6 0.0 copy-start.3
  314.6 2.0 copy-done.3
  316.6 0.0 copy-done.6
  316.6 0.0 copy-done.7
  316.6 0.0 copy-start.10
  316.6 0.0 copy-start.8
  316.6 1.9 fusion.41
  318.5 0.0 all-gather.3.cloned.1.call-update
  318.6 0.0 copy-done.10
  318.6 18.6 %all-gather = s32[8,1,128]{2,1,0:T(1,128)S(1)} all-gather(s32[1,1,128]{2,1,0:T(1,128)S(1)} %bitcast.48), channel_id=1, replica_groups=mesh['shard'=4,'tensor'=4,'section'=2] {'shard','section'}, dimensions={0}, use_global_device_ids=true | all-gather | bytes 4608 | tf_op jit(solution)/shard_map/all_gather | solution.py:78
  337.2 0.0 copy-done.8
  337.2 33.2 %all_gather.11 = bf16[1024,256]{1,0:T(8,128)(2,1)S(1)} all-gather(bf16[128,256]{1,0:T(8,128)(2,1)S(1)} %copy-done.8), channel_id=1, replica_groups=mesh['shard'=4,'tensor'=4,'section'=2] {'shard','section'}, dimensions={0}, use_global_device_ids=true | all-gather | bytes 589824 | tf_op jit(solution)/shard_map/all_gather | solution.py:77
  370.3 0.0 copy-start.5
  370.3 8.3 %scatter_custom_fusion = f32[4096,256]{1,0:T(8,128)} fusion(s32[1024]{0:T(1024)S(1)} %compare_select_fusion, f32[]{:T(128)} %constant.16.clone.1, bf16[1024,256]{1,0:T(8,128)(2,1)S(1)} %all_gather.11), kind=kCustom, calls=%fused_computation.7 | custom fusion | flops 524288 | bytes 4718596 | tf_op jit(solution)/shard_map/scatter-add | solution.py:86
  378.6 0.0 copy-start.2
  378.6 0.0 copy-start.4
  378.6 4.8 %subtract_convert_fusion = bf16[4096,256]{1,0:T(8,128)(2,1)} fusion(f32[4096,256]{1,0:T(8,128)} %scatter_custom_fusion, bf16[4096,256]{1,0:T(8,128)(2,1)} %param.17), kind=kLoop, calls=%fused_computation.5 | loop fusion | flops 4194304 | bytes 8388608 | tf_op jit(solution)/shard_map/convert_element_type | solution.py:88
  383.4 0.0 copy-done.5
  383.4 0.7 multiply_bitcast_fusion
  384.1 0.0 copy-done.2
  384.1 0.6 copy-done.4
  384.7 3.6 subtract_bitcast_fusion
  388.3 0.0 all-gather.3.cloned.1.call-done
  388.3 3.1 copy.21
  (2 shorter events, 0.0 us)
Async XLA Ops:
  7.2 9.4 %copy-start = (f32[1,32,1024]{2,1,0:T(8,128)S(1)}, f32[1,32,1024]{2,1,0:T(8,128)}, u32[]{:S(2)}) copy-start(f32[1,32,1024]{2,1,0:T(8,128)} %param.13) | copy-start | bytes 393220
  7.2 103.9 %all-reduce.5.cloned.1.call-start = ((), (), s32[]{:S(2)}) async-start(), calls=%async_computation | async-start | bytes 262144 | tf_op jit(solution)/shard_map/psum | solution.py:46
  7.2 9.3 %copy-start.1 = (f32[1,1,1024,1024]{3,2,1,0:T(8,128)S(1)}, f32[1,1,1024,1024]{3,2,1,0:T(8,128)}, u32[]{:S(2)}) copy-start(f32[1,1,1024,1024]{3,2,1,0:T(8,128)} %param.12) | copy-start | bytes 12582916
  16.5 94.6 %copy-start.9 = (f32[1,2,32,32]{3,2,1,0:T(8,128)S(1)}, f32[1,2,32,32]{3,2,1,0:T(8,128)}, u32[]{:S(2)}) copy-start(f32[1,2,32,32]{3,2,1,0:T(8,128)} %param.14) | copy-start | bytes 24580
  21.3 134.2 %all-reduce.7.cloned.1.call-start = ((), (), s32[]{:S(2)}) async-start(), calls=%async_computation.1 | async-start | bytes 262144 | tf_op jit(solution)/shard_map/psum | solution.py:51
  119.2 129.8 %all-reduce.9.cloned.1.call-start = ((), (), s32[]{:S(2)}) async-start(), calls=%async_computation.2 | async-start | bytes 262144 | tf_op jit(solution)/shard_map/psum | solution.py:46
  162.3 131.3 %all-reduce.11.cloned.1.call-start = ((), (), s32[]{:S(2)}) async-start(), calls=%async_computation.3 | async-start | bytes 262144 | tf_op jit(solution)/shard_map/psum | solution.py:51
  251.6 65.0 %copy-start.6 = (f32[1,256,1024]{2,1,0:T(8,128)S(1)}, f32[1,256,1024]{2,1,0:T(8,128)}, u32[]{:S(2)}) copy-start(f32[1,256,1024]{2,1,0:T(8,128)} %param.16) | copy-start | bytes 3145732
  257.3 131.1 %all-gather.3.cloned.1.call-start = ((), (), s32[]{:S(2)}) async-start(), calls=%async_computation.4 | async-start | bytes 2621440 | tf_op jit(solution)/shard_map/all_gather | solution.py:71
  310.1 6.5 %copy-start.7 = (f32[1,256,1024]{2,1,0:T(8,128)S(1)}, f32[1,256,1024]{2,1,0:T(8,128)}, u32[]{:S(2)}) copy-start(f32[1,256,1024]{2,1,0:T(8,128)} %param.15) | copy-start | bytes 3145732
  314.6 2.0 copy-start.3
  316.6 2.0 copy-start.10
  316.6 20.6 %copy-start.8 = (bf16[128,256]{1,0:T(8,128)(2,1)S(1)}, bf16[128,256]{1,0:T(8,128)(2,1)}, u32[]{:S(2)}) copy-start(bf16[128,256]{1,0:T(8,128)(2,1)} %param.19) | copy-start | bytes 196612
  370.3 13.1 %copy-start.5 = (f32[32,1024]{1,0:T(8,128)S(1)}, f32[32,1024]{1,0:T(8,128)}, u32[]{:S(2)}) copy-start(f32[32,1024]{1,0:T(8,128)} %all-reduce.11.cloned.1.call-done) | copy-start | bytes 393220
  378.6 5.5 %copy-start.2 = (f32[1,1,1024,1024]{3,2,1,0:T(8,128)S(1)}, f32[1,1,1024,1024]{3,2,1,0:T(8,128)}, u32[]{:S(2)}) copy-start(f32[1,1,1024,1024]{3,2,1,0:T(8,128)} %param.12) | copy-start | bytes 12582916
  378.6 6.1 %copy-start.4 = (f32[1024,1024]{1,0:T(8,128)S(1)}, f32[1024,1024]{1,0:T(8,128)}, u32[]{:S(2)}) copy-start(f32[1024,1024]{1,0:T(8,128)} %copy-done.3) | copy-start | bytes 12582916
Sparse Core Ops, SparseCore 0:
  21.4 89.6 all-reduce.4
  119.4 36.0 all-reduce.6
  162.4 86.6 all-reduce.8
  257.4 36.1 all-reduce.10
  318.7 49.5 all-gather.2
where the time goes:
time: 398 us
  waiting for transfers between devices  249 us (63%)
  blocking collectives  65.7 us (17%)
  matrix products  42.2 us (11%)
  other arithmetic  19.3 us (5%)
  between operations  16 us (4%)
  local copies, waits for them, and re-layouts  5.77 us (1%)
    psum x2, waiting for transfers between devices, on_device(): left_sum = lax.psum(left_part, ('shard', 'tensor'))  176 us
    psum x2, waiting for transfers between devices, on_device(): right_part = lax.psum(right_local, 'shard') / shards  72.2 us
    all_gather x1, blocking collectives, on_device(): lax.all_gather(touched_grads, ('shard', 'section'), axis=0, tiled=True)  33.2 us
    all_gather x1, blocking collectives, on_device(): lax.all_gather(touched_ids, ('shard', 'section'), axis=0, tiled=True)  18.6 us
    psum x1, blocking collectives, on_device(): lax.psum(jnp.sum(gram_left * gram_right), ('tensor', 'section'))  14 us
    dot_general x2, matrix products, on_device(): lax.dot_general(right_part, corrected, (((1,), (1,)), ((), ())), precisio...  11.4 us
    dot_general x2, matrix products, on_device(): right_local = jnp.dot(left_unit, corrected, precision=highest)  11.2 us
    dot_general x1, matrix products, on_device(): lax.dot_general(out_grads[0], hidden_acts[0], (((0,), (0,)), ((), ())), p...  9.28 us
  transfers between devices with their start and end apart: 5, of which 4 were waited for; matrix products, arithmetic and copies ran while one was open for 4% of the time, Pallas kernels for 0%

commit v1 on v0

--- a/solution.py
+++ b/solution.py
@@ -12,6 +12,24 @@
 embed_rate = 0.25
 clip_level = 0.03
 highest = lax.Precision.HIGHEST
+
+
+def collect(array, axis, dim):
+    ways, here, step = (lax.axis_size(axis), lax.axis_index(axis), array.shape[dim])
+    lengths = [n * ways if d == dim else n for d, n in enumerate(array.shape)]
+    full = lax.dynamic_update_slice_in_dim(
+        jnp.zeros(lengths, array.dtype), array, here * step, axis=dim
+    )
+    going_up = going_down = array
+    for far in range(1, ways // 2 + 1):
+        going_up = lax.ppermute(going_up, axis, [(d, (d + 1) % ways) for d in range(ways)])
+        full = lax.dynamic_update_slice_in_dim(full, going_up, (here - far) % ways * step, axis=dim)
+        if 2 * far < ways:
+            going_down = lax.ppermute(going_down, axis, [(d, (d - 1) % ways) for d in range(ways)])
+            full = lax.dynamic_update_slice_in_dim(
+                full, going_down, (here + far) % ways * step, axis=dim
+            )
+    return full
 
 
 def on_device(
@@ -75,7 +93,7 @@
     first_row = lax.axis_index(("shard", "section")) * vocab_rows
     recv_rows, recv_ids = (
         lax.all_gather(touched_grads, ("shard", "section"), axis=0, tiled=True),
-        lax.all_gather(touched_ids, ("shard", "section"), axis=0, tiled=True),
+        collect(touched_ids, ("shard", "section"), 0),
     )
     local_index = recv_ids - first_row
     inside = (local_index >= 0) & (local_index < vocab_rows)

time: 398 us -> 403 us (1.013)
  blocking collectives: 65.7 us -> 47.1 us
  starting transfers between devices: 0.39 us -> 12.3 us
  waiting for transfers between devices: 249 us -> 258 us
    all_gather x1 -> x0, blocking collectives: 18.6 us -> none  [on_device(): lax.all_gather(touched_ids, ('shard', 'section'), axis=0, tiled=True)]
    ppermute x0 -> x7, starting transfers between devices: none -> 11.9 us  [the longest x3 10.1 us: collect(): lax.ppermute(going_down, axis, [(d, (d - 1) % ways) for d in range(ways)])]
    ppermute x0 -> x7, waiting for transfers between devices: none -> 7.9 us  [the longest x4 7.89 us: collect(): lax.ppermute(going_up, axis, [(d, (d + 1) % ways) for d in range(ways)])]
  transfers between devices with their start and end apart: 5 -> 12, of which waited for: 4 -> 7; matrix products, arithmetic and copies ran while one was open for 4% -> 5% of each run, Pallas kernels for 0% -> 0%
where the time goes in v1:
time: 403 us
  waiting for transfers between devices  258 us (64%)
  blocking collectives  47.1 us (12%)
  matrix products  42.1 us (10%)
  other arithmetic  19.3 us (5%)
  between operations  16 us (4%)
  starting transfers between devices  12.3 us (3%)
  local copies, waits for them, and re-layouts  7.37 us (2%)
    psum x2, waiting for transfers between devices, on_device(): left_sum = lax.psum(left_part, ('shard', 'tensor'))  179 us
    psum x2, waiting for transfers between devices, on_device(): right_part = lax.psum(right_local, 'shard') / shards  71 us
    all_gather x1, blocking collectives, on_device(): lax.all_gather(touched_grads, ('shard', 'section'), axis=0, tiled=True)  33.1 us
    psum x1, blocking collectives, on_device(): lax.psum(jnp.sum(gram_left * gram_right), ('tensor', 'section'))  14 us
    dot_general x2, matrix products, on_device(): right_local = jnp.dot(left_unit, corrected, precision=highest)  11.2 us
    dot_general x2, matrix products, on_device(): lax.dot_general(right_part, corrected, (((1,), (1,)), ((), ())), precisio...  10.9 us
    ppermute x3, starting transfers between devices, collect(): lax.ppermute(going_down, axis, [(d, (d - 1) % ways) for d in range(ways)])  10.1 us
    dot_general x1, matrix products, on_device(): lax.dot_general(out_grads[0], hidden_acts[0], (((0,), (0,)), ((), ())), p...  9.28 us
  transfers between devices with their start and end apart: 12, of which 7 were waited for; matrix products, arithmetic and copies ran while one was open for 5% of the time, Pallas kernels for 0%

profile of v1, /device:TPU:0, one launch (start us, length us, event | category | flops | bytes accessed | tf_op | source)
XLA Modules:
  0.0 402.6 jit_solution(835239645425002063)
XLA Ops:
  7.2 0.0 copy-start
  7.2 0.0 all-reduce.5.cloned.1.call-start
  7.2 0.0 copy-start.1
  7.2 9.3 %fusion.5 = bf16[1024,1024]{1,0:T(8,128)(2,1)S(1)} fusion(bf16[1,2560,1024]{2,1,0:T(8,128)(2,1)} %param.10, bf16[1,2560,1024]{2,1,0:T(8,128)(2,1)} %param.11), kind=kOutput, calls=%fused_computation.9 | convolution fusion | flops 5369757696 | bytes 12582912 | tf_op jit(solution)/shard_map/dot_general | solution.py:48
  16.5 0.0 copy-start.9
  16.6 4.2 %convolution_bitcast_fusion = f32[32,1024]{0,1:T(8,128)} fusion(f32[1,32,1024]{2,1,0:T(8,128)S(1)} %copy-done, f32[1,1,1024,1024]{3,2,1,0:T(8,128)S(1)} %copy-done.1, bf16[1024,1024]{1,0:T(8,128)(2,1)S(1)} %fusion.5), kind=kOutput, calls=%fused_computation.10 | convolution fusion | flops 404750336 | bytes 6553600 | tf_op jit(solution)/shard_map/dot_general | solution.py:57
  20.7 0.0 all-reduce.5.cloned.1.call-update
  20.8 0.0 all-reduce.7.cloned.1.call-start
  20.8 92.9 %all-reduce.5.cloned.1.call-done = f32[32,1024]{0,1:T(8,128)} async-done(((f32[32,1024]{0,1:T(8,128)}), f32[32,1024]{0,1:T(8,128)}) %all-reduce.5.cloned.1.call-update) | async-done | bytes 131088 | tf_op jit(solution)/shard_map/psum | solution.py:64
  113.7 2.3 multiply_reduce_fusion.1
  116.7 5.6 %fusion.15 = f32[32,1024]{1,0:T(8,128)} fusion(f32[1024,32]{0,1:T(8,128)S(1)} %get-tuple-element.10, f32[]{:T(128)S(6)} %rsqrt.7, f32[1,1,1024,1024]{3,2,1,0:T(8,128)} %param.12, bf16[1024,1024]{1,0:T(8,128)(2,1)S(1)} %fusion.5), kind=kOutput, calls=%fused_computation.20 | convolution fusion | flops 404783104 | bytes 6553604 | tf_op jit(solution)/shard_map/dot_general | solution.py:68
  122.3 0.0 all-reduce.7.cloned.1.call-update
  122.3 0.0 all-reduce.9.cloned.1.call-start
  122.3 35.0 %all-reduce.7.cloned.1.call-done = f32[32,1024]{1,0:T(8,128)} async-done(((f32[32,1024]{1,0:T(8,128)}), f32[32,1024]{1,0:T(8,128)}) %all-reduce.7.cloned.1.call-update) | async-done | bytes 131088 | tf_op jit(solution)/shard_map/psum | solution.py:69
  157.3 6.8 %fusion.13 = f32[32,1024]{1,0:T(8,128)} fusion(f32[32,1024]{1,0:T(8,128)} %all-reduce.7.cloned.1.call-done, f32[1,1,1024,1024]{3,2,1,0:T(8,128)} %param.12, bf16[1024,1024]{1,0:T(8,128)(2,1)S(1)} %fusion.5), kind=kOutput, calls=%fused_computation.18 | convolution fusion | flops 404783104 | bytes 6553600 | tf_op jit(solution)/shard_map/dot_general | solution.py:57
  164.1 0.0 all-reduce.9.cloned.1.call-update
  164.1 0.2 all-reduce.11.cloned.1.call-start
  164.4 86.6 %all-reduce.9.cloned.1.call-done = f32[32,1024]{1,0:T(8,128)} async-done(((f32[32,1024]{1,0:T(8,128)}), f32[32,1024]{1,0:T(8,128)}) %all-reduce.9.cloned.1.call-update) | async-done | bytes 131088 | tf_op jit(solution)/shard_map/psum | solution.py:64
  251.0 1.8 multiply_reduce_fusion
  253.5 0.0 copy-start.6
  253.5 5.6 %fusion.23 = f32[32,1024]{1,0:T(8,128)} fusion(f32[1024,32]{0,1:T(8,128)S(1)} %get-tuple-element.12, f32[]{:T(128)S(6)} %rsqrt.8, f32[1,1,1024,1024]{3,2,1,0:T(8,128)} %param.12, bf16[1024,1024]{1,0:T(8,128)(2,1)S(1)} %fusion.5), kind=kOutput, calls=%fused_computation.30 | convolution fusion | flops 404783104 | bytes 6553604 | tf_op jit(solution)/shard_map/dot_general | solution.py:68
  259.2 0.0 all-reduce.11.cloned.1.call-update
  259.2 0.0 all-gather.2.cloned.1.call-start
  259.2 0.2 fusion.20
  259.5 36.0 %all-reduce.11.cloned.1.call-done = f32[32,1024]{1,0:T(8,128)} async-done(((f32[32,1024]{1,0:T(8,128)}), f32[32,1024]{1,0:T(8,128)}) %all-reduce.11.cloned.1.call-update) | async-done | bytes 131088 | tf_op jit(solution)/shard_map/psum | solution.py:69
  295.5 1.8 fusion.11
  297.3 14.0 %psum.39 = f32[]{:T(128)} all-reduce(f32[]{:T(128)} %fusion.11), channel_id=1, replica_groups=mesh['shard'=4,'tensor'=4,'section'=2] {'tensor','section'}, use_global_device_ids=true, to_apply=%region_7.0 | all-reduce | flops 1 | bytes 8 | tf_op jit(solution)/shard_map/psum | solution.py:72
  312.0 0.0 copy-start.7
  312.0 4.5 %fusion.18 = f32[1024,1024]{1,0:T(8,128)S(1)} fusion(f32[32,1024]{1,0:T(8,128)} %all-reduce.11.cloned.1.call-done, f32[1024,32]{0,1:T(8,128)S(1)} %get-tuple-element.12, f32[]{:T(128)S(6)} %rsqrt.8), kind=kOutput, calls=%fused_computation.25 | convolution fusion | flops 402718720 | bytes 4456452 | tf_op jit(solution)/shard_map/dot_general | solution.py:73
  316.5 0.0 copy-start.3
  316.5 2.0 copy-done.3
  318.5 0.0 copy-done.6
  318.5 1.9 fusion.41
  320.4 0.0 all-gather.2.cloned.1.call-update
  320.5 0.0 copy-done.10
  320.5 2.4 collective-permute-start.1
  322.8 0.0 collective-permute-start
  322.8 33.1 %all_gather.7 = bf16[1024,256]{1,0:T(8,128)(2,1)S(1)} all-gather(bf16[128,256]{1,0:T(8,128)(2,1)S(1)} %copy-done.8), channel_id=1, replica_groups=mesh['shard'=4,'tensor'=4,'section'=2] {'shard','section'}, dimensions={0}, use_global_device_ids=true | all-gather | bytes 589824 | tf_op jit(solution)/shard_map/all_gather | solution.py:95
  355.9 0.0 collective-permute-done
  355.9 1.8 collective-permute-start.2
  357.7 0.0 collective-permute-done.1
  357.7 3.0 collective-permute-start.3
  360.7 1.5 collective-permute-done.2
  362.2 0.0 collective-permute-start.4
  362.2 0.0 collective-permute-done.3
  362.2 4.8 %collective-permute-start.5 = (s32[128]{0:T(128)S(1)}, s32[128]{0:T(128)S(1)}, u32[]{:S(2)}, u32[]{:S(2)}) collective-permute-start(s32[128]{0:T(128)S(1)} %collective-permute-done.3), channel_id=1, source_target_pairs={{0,25},{1,0},{8,1},{9,8},{16,9},{17,16},{24,17},{25,24},{2,27},{3,... | collective-permute-start | bytes 1544 | tf_op jit(solution)/shard_map/ppermute | solution.py:28
  367.0 1.6 collective-permute-done.4
  368.6 0.0 collective-permute-start.6
  368.6 0.2 dynamic_update_slice.24
  368.8 0.2 dynamic_update_slice.25
  369.0 0.2 dynamic_update_slice.26
  369.2 0.2 dynamic_update_slice.27
  369.4 0.2 dynamic_update_slice.28
  369.6 0.2 dynamic_update_slice.29
  369.8 0.0 collective-permute-done.5
  369.8 0.2 dynamic_update_slice.30
  370.0 4.8 %collective-permute-done.6 = s32[128]{0:T(128)S(1)} collective-permute-done((s32[128]{0:T(128)S(1)}, s32[128]{0:T(128)S(1)}, u32[]{:S(2)}, u32[]{:S(2)}) %collective-permute-start.6) | collective-permute-done | bytes 544 | tf_op jit(solution)/shard_map/ppermute | solution.py:25
  374.8 0.2 dynamic_update_slice.31
  375.0 8.3 %scatter_custom_fusion = f32[4096,256]{1,0:T(8,128)} fusion(s32[1024]{0:T(1024)S(1)} %compare_select_fusion, f32[]{:T(128)} %constant.72.clone.1, bf16[1024,256]{1,0:T(8,128)(2,1)S(1)} %all_gather.7), kind=kCustom, calls=%fused_computation.7 | custom fusion | flops 524288 | bytes 4718596 | tf_op jit(solution)/shard_map/scatter-add | solution.py:104
  383.3 4.8 %subtract_convert_fusion = bf16[4096,256]{1,0:T(8,128)(2,1)} fusion(f32[4096,256]{1,0:T(8,128)} %scatter_custom_fusion, bf16[4096,256]{1,0:T(8,128)(2,1)} %param.17), kind=kLoop, calls=%fused_computation.5 | loop fusion | flops 4194304 | bytes 8388608 | tf_op jit(solution)/shard_map/convert_element_type | solution.py:106
  388.1 0.7 multiply_bitcast_fusion
  388.8 0.6 copy-done.4
  389.4 3.6 subtract_bitcast_fusion
  393.0 3.1 copy.29
  (15 shorter events, 0.0 us)
Async XLA Ops:
  7.2 9.4 %copy-start = (f32[1,32,1024]{2,1,0:T(8,128)S(1)}, f32[1,32,1024]{2,1,0:T(8,128)}, u32[]{:S(2)}) copy-start(f32[1,32,1024]{2,1,0:T(8,128)} %param.13) | copy-start | bytes 393220
  7.2 106.5 %all-reduce.5.cloned.1.call-start = ((), (), s32[]{:S(2)}) async-start(), calls=%async_computation | async-start | bytes 1048576 | tf_op jit(solution)/shard_map/psum | solution.py:64
  7.2 9.3 %copy-start.1 = (f32[1,1,1024,1024]{3,2,1,0:T(8,128)S(1)}, f32[1,1,1024,1024]{3,2,1,0:T(8,128)}, u32[]{:S(2)}) copy-start(f32[1,1,1024,1024]{3,2,1,0:T(8,128)} %param.12) | copy-start | bytes 12582916
  16.5 97.1 %copy-start.9 = (f32[1,2,32,32]{3,2,1,0:T(8,128)S(1)}, f32[1,2,32,32]{3,2,1,0:T(8,128)}, u32[]{:S(2)}) copy-start(f32[1,2,32,32]{3,2,1,0:T(8,128)} %param.14) | copy-start | bytes 24580
  20.8 136.6 %all-reduce.7.cloned.1.call-start = ((), (), s32[]{:S(2)}) async-start(), calls=%async_computation.1 | async-start | bytes 262144 | tf_op jit(solution)/shard_map/psum | solution.py:69
  122.3 128.7 %all-reduce.9.cloned.1.call-start = ((), (), s32[]{:S(2)}) async-start(), calls=%async_computation.2 | async-start | bytes 262144 | tf_op jit(solution)/shard_map/psum | solution.py:64
  164.1 131.4 %all-reduce.11.cloned.1.call-start = ((), (), s32[]{:S(2)}) async-start(), calls=%async_computation.3 | async-start | bytes 262144 | tf_op jit(solution)/shard_map/psum | solution.py:69
  253.5 65.0 %copy-start.6 = (f32[1,256,1024]{2,1,0:T(8,128)S(1)}, f32[1,256,1024]{2,1,0:T(8,128)}, u32[]{:S(2)}) copy-start(f32[1,256,1024]{2,1,0:T(8,128)} %param.16) | copy-start | bytes 3145732
  259.2 133.8 %all-gather.2.cloned.1.call-start = ((), (), s32[]{:S(2)}) async-start(), calls=%async_computation.4 | async-start | bytes 2621440 | tf_op jit(solution)/shard_map/all_gather | solution.py:89
  312.0 6.5 %copy-start.7 = (f32[1,256,1024]{2,1,0:T(8,128)S(1)}, f32[1,256,1024]{2,1,0:T(8,128)}, u32[]{:S(2)}) copy-start(f32[1,256,1024]{2,1,0:T(8,128)} %param.15) | copy-start | bytes 3145732
  316.5 2.0 copy-start.3
  318.5 1.9 copy-start.10
  318.5 4.3 %copy-start.8 = (bf16[128,256]{1,0:T(8,128)(2,1)S(1)}, bf16[128,256]{1,0:T(8,128)(2,1)}, u32[]{:S(2)}) copy-start(bf16[128,256]{1,0:T(8,128)(2,1)} %param.19) | copy-start | bytes 196612
  320.5 37.3 %collective-permute-start.1 = (s32[128]{0:T(128)S(1)}, s32[128]{0:T(128)S(1)}, u32[]{:S(2)}, u32[]{:S(2)}) collective-permute-start(s32[128]{0:T(128)S(1)} %copy-done.10), channel_id=1, source_target_pairs={{0,25},{1,0},{8,1},{9,8},{16,9},{17,16},{24,17},{25,24},{2,27},{3,... | collective-permute-start | bytes 1544 | tf_op jit(solution)/shard_map/ppermute | solution.py:28
  322.8 33.1 %collective-permute-start = (s32[128]{0:T(128)S(1)}, s32[128]{0:T(128)S(1)}, u32[]{:S(2)}, u32[]{:S(2)}) collective-permute-start(s32[128]{0:T(128)S(1)} %copy-done.10), channel_id=1, source_target_pairs={{0,1},{1,8},{8,9},{9,16},{16,17},{17,24},{24,25},{25,0},{2,3},{3,1... | collective-permute-start | bytes 1544 | tf_op jit(solution)/shard_map/ppermute | solution.py:25
  355.9 6.3 %collective-permute-start.2 = (s32[128]{0:T(128)S(1)}, s32[128]{0:T(128)S(1)}, u32[]{:S(2)}, u32[]{:S(2)}) collective-permute-start(s32[128]{0:T(128)S(1)} %collective-permute-done), channel_id=1, source_target_pairs={{0,1},{1,8},{8,9},{9,16},{16,17},{17,24},{24,25},{25,0},{2,3},{3,1... | collective-permute-start | bytes 1544 | tf_op jit(solution)/shard_map/ppermute | solution.py:25
  357.7 4.5 %collective-permute-start.3 = (s32[128]{0:T(128)S(1)}, s32[128]{0:T(128)S(1)}, u32[]{:S(2)}, u32[]{:S(2)}) collective-permute-start(s32[128]{0:T(128)S(1)} %collective-permute-done.1), channel_id=1, source_target_pairs={{0,25},{1,0},{8,1},{9,8},{16,9},{17,16},{24,17},{25,24},{2,27},{3,... | collective-permute-start | bytes 1544 | tf_op jit(solution)/shard_map/ppermute | solution.py:28
  362.2 6.3 %collective-permute-start.4 = (s32[128]{0:T(128)S(1)}, s32[128]{0:T(128)S(1)}, u32[]{:S(2)}, u32[]{:S(2)}) collective-permute-start(s32[128]{0:T(128)S(1)} %collective-permute-done.2), channel_id=1, source_target_pairs={{0,1},{1,8},{8,9},{9,16},{16,17},{17,24},{24,25},{25,0},{2,3},{3,1... | collective-permute-start | bytes 1544 | tf_op jit(solution)/shard_map/ppermute | solution.py:25
  362.2 7.6 %collective-permute-start.5 = (s32[128]{0:T(128)S(1)}, s32[128]{0:T(128)S(1)}, u32[]{:S(2)}, u32[]{:S(2)}) collective-permute-start(s32[128]{0:T(128)S(1)} %collective-permute-done.3), channel_id=1, source_target_pairs={{0,25},{1,0},{8,1},{9,8},{16,9},{17,16},{24,17},{25,24},{2,27},{3,... | collective-permute-start | bytes 1544 | tf_op jit(solution)/shard_map/ppermute | solution.py:28
  368.6 6.2 %collective-permute-start.6 = (s32[128]{0:T(128)S(1)}, s32[128]{0:T(128)S(1)}, u32[]{:S(2)}, u32[]{:S(2)}) collective-permute-start(s32[128]{0:T(128)S(1)} %collective-permute-done.4), channel_id=1, source_target_pairs={{0,1},{1,8},{8,9},{9,16},{16,17},{17,24},{24,25},{25,0},{2,3},{3,1... | collective-permute-start | bytes 1544 | tf_op jit(solution)/shard_map/ppermute | solution.py:25
  375.0 13.1 %copy-start.5 = (f32[32,1024]{1,0:T(8,128)S(1)}, f32[32,1024]{1,0:T(8,128)}, u32[]{:S(2)}) copy-start(f32[32,1024]{1,0:T(8,128)} %all-reduce.11.cloned.1.call-done) | copy-start | bytes 393220
  383.3 5.5 %copy-start.2 = (f32[1,1,1024,1024]{3,2,1,0:T(8,128)S(1)}, f32[1,1,1024,1024]{3,2,1,0:T(8,128)}, u32[]{:S(2)}) copy-start(f32[1,1,1024,1024]{3,2,1,0:T(8,128)} %param.12) | copy-start | bytes 12582916
  383.3 6.1 %copy-start.4 = (f32[1024,1024]{1,0:T(8,128)S(1)}, f32[1024,1024]{1,0:T(8,128)}, u32[]{:S(2)}) copy-start(f32[1024,1024]{1,0:T(8,128)} %copy-done.3) | copy-start | bytes 12582916
Sparse Core Ops, SparseCore 0:
  20.9 92.7 all-reduce.4
  122.4 34.8 all-reduce.6
  164.2 86.6 all-reduce.8
  259.3 36.1 all-reduce.10
  320.6 48.7 all-gather.1
